TPU v7x, 32 devices: a whole 2x2x4 slice. The times are simulated.
32 devices in a mesh: row: 8 (over y, x, core), col: 4 (over z).
Axes of the slice: x: 2, y: 2, z: 4, core: 2. Of those that a mesh axis runs over, the one named last changes fastest.
Arguments:
- pair: bfloat16 [256, 256, 128], P('row', 'col'), may hold values from -6 to 6
- cotangent: bfloat16 [256, 256, 128], P('row', 'col'), may hold values from -6 to 6
- length: int32 [1], replicated, may hold values from 128 to 256
- norm_gain: float32 [128], replicated, may hold values from 0.1 to 1.9
- norm_bias: float32 [128], replicated, may hold values from -1.5 to 1.5
- left_weight: bfloat16 [128, 256], replicated, may hold values from -0.5 to 0.5
- right_weight: bfloat16 [128, 256], replicated, may hold values from -0.5 to 0.5
- gate_weight: bfloat16 [128, 128], replicated, may hold values from -0.5 to 0.5
- out_gain: float32 [128], replicated, may hold values from 0.1 to 1.9
- out_bias: float32 [128], replicated, may hold values from -2 to 2
- out_weight: bfloat16 [128, 128], replicated, may hold values from -0.5 to 0.5
Outputs:
- update: bfloat16 [256, 256, 128], P('row', 'col')
- grad_pair: bfloat16 [256, 256, 128], P('row', 'col')
- grad_left: float32 [128, 256], replicated
- grad_right: float32 [128, 256], replicated
- grad_gating: float32 [128, 128], replicated
- grad_output: float32 [128, 128], replicated
- grad_norms: float32 [4, 128], replicated
Inputs may be any that keep to these rules, and one draw needn't show every extreme that they name: Tokens at positions 255 down to length are padding.
All inputs are finite; a program needn't handle non-finite values.
Results may differ from a plain program's by a relative error of at most 0.014.
Values may be sent and summed in bfloat16 or wider, within the bound.
No kernel may reach another device: no remote copies, remote signals or barrier semaphores. Data moves between devices by JAX's collectives and lax.ppermute only.
A program may use at most 128 MiB of HBM per device.

v0:
```python
import jax
import jax.numpy as jnp
from jax import lax
from jax.sharding import PartitionSpec as P

EPS = 1e-05


def broadcast(block, axis, holder):
    block = jnp.where(lax.axis_index(axis) == holder, block, jnp.zeros_like(block))
    return lax.psum(block, axis)


def normalize(values):
    center = values - jnp.mean(values, axis=-1, keepdims=True)
    inverse = lax.rsqrt(jnp.mean(center * center, axis=-1, keepdims=True) + EPS)
    return (center * inverse, inverse)


def gating(panel, weight, first_ok, second_ok, hidden):
    projected = jnp.einsum("ikc,ch->ikh", panel, weight, preferred_element_type=jnp.float32)
    values = projected[..., :hidden]
    sigmoid_val = jax.nn.sigmoid(projected[..., hidden:])
    pad_mask = (first_ok[:, None] & second_ok[None, :]).astype(jnp.float32)[..., None]
    return ((pad_mask * sigmoid_val * values).astype(jnp.bfloat16), values, sigmoid_val, pad_mask)


def push_back(partial_value, values, sigmoid_val, pad_mask, weight, panel):
    combined = jnp.concatenate(
        [
            partial_value * pad_mask * sigmoid_val,
            partial_value * pad_mask * values * sigmoid_val * (1.0 - sigmoid_val),
        ],
        axis=-1,
    ).astype(jnp.bfloat16)
    panel_grad = jnp.einsum("ikh,ch->ikc", combined, weight, preferred_element_type=jnp.float32)
    weight_grad = jnp.einsum("ikc,ikh->ch", panel, combined, preferred_element_type=jnp.float32)
    return (panel_grad, weight_grad)


def per_device(
    pair,
    cotangent,
    length,
    norm_gain,
    norm_bias,
    left_weight,
    right_weight,
    gate_weight,
    out_gain,
    out_bias,
    out_weight,
):
    row_index = lax.axis_index("row")
    col_index = lax.axis_index("col")
    n_row = lax.axis_size("row")
    n_col = lax.axis_size("col")
    per_col = n_row // n_col
    rows_dev = pair.shape[0]
    cols_dev = pair.shape[1]
    tokens = rows_dev * n_row
    hidden = out_weight.shape[0]
    pair_hat, pair_scale = normalize(pair.astype(jnp.float32))
    normed = (pair_hat * norm_gain + norm_bias).astype(jnp.bfloat16)
    real_count = length[0]
    second_ok = jnp.arange(tokens, dtype=jnp.int32) < real_count
    own_ok = row_index * rows_dev + jnp.arange(rows_dev, dtype=jnp.int32) < real_count
    partner_ok = col_index * cols_dev + jnp.arange(cols_dev, dtype=jnp.int32) < real_count
    left_tile, left_val, left_sig, tile_mask = gating(
        normed, left_weight, own_ok, partner_ok, hidden
    )
    right_tile, right_val, right_sig, unused_mask = gating(
        normed, right_weight, own_ok, partner_ok, hidden
    )
    row_panel = lax.all_gather(normed, "col", axis=1, tiled=True)
    pieces = []
    for member in range(per_col):
        pieces.append(broadcast(row_panel, "row", col_index * per_col + member))
    col_panel = jnp.concatenate(pieces, axis=0)
    left_act = gating(row_panel, left_weight, own_ok, second_ok, hidden)[0]
    right_act = gating(col_panel, right_weight, partner_ok, second_ok, hidden)[0]
    tri = jnp.einsum("ikh,jkh->ijh", left_act, right_act, preferred_element_type=jnp.float32)
    tri_hat, tri_scale = normalize(tri)
    tri_normed = (tri_hat * out_gain + out_bias).astype(jnp.bfloat16)
    outer_val = jnp.einsum(
        "ijh,hc->ijc", tri_normed, out_weight, preferred_element_type=jnp.float32
    )
    gate_val = jax.nn.sigmoid(
        jnp.einsum("ijc,cd->ijd", normed, gate_weight, preferred_element_type=jnp.float32)
    )
    update = (gate_val * outer_val).astype(jnp.bfloat16)
    upstream = cotangent.astype(jnp.float32)
    outer_grad = (upstream * gate_val).astype(jnp.bfloat16)
    gate_grad = (upstream * outer_val * gate_val * (1.0 - gate_val)).astype(jnp.bfloat16)
    grad_output = jnp.einsum(
        "ijh,ijc->hc", tri_normed, outer_grad, preferred_element_type=jnp.float32
    )
    grad_gating = jnp.einsum("ijc,ijd->cd", normed, gate_grad, preferred_element_type=jnp.float32)
    tnorm_grad = jnp.einsum(
        "ijc,hc->ijh", outer_grad, out_weight, preferred_element_type=jnp.float32
    )
    hat_grad = tnorm_grad * out_gain
    tri_grad = (
        tri_scale
        * (
            hat_grad
            - jnp.mean(hat_grad, axis=-1, keepdims=True)
            - tri_hat * jnp.mean(hat_grad * tri_hat, axis=-1, keepdims=True)
        )
    ).astype(jnp.bfloat16)
    row_partial = jnp.einsum(
        "ijh,jkh->ikh", tri_grad, right_act, preferred_element_type=jnp.float32
    )
    col_partial = jnp.einsum("ijh,ikh->jkh", tri_grad, left_act, preferred_element_type=jnp.float32)
    row_part = lax.psum_scatter(
        row_partial.astype(jnp.bfloat16), "col", scatter_dimension=1, tiled=True
    ).astype(jnp.float32)
    summed = lax.psum_scatter(
        col_partial.astype(jnp.bfloat16), "row", scatter_dimension=0, tiled=True
    )
    slab = summed[None]
    received = lax.all_to_all(slab, "col", split_axis=2, concat_axis=0, tiled=True)
    select = (jnp.arange(per_col, dtype=jnp.int32) == row_index // n_col).astype(jnp.bfloat16)
    spread = (received[:, None] * select[None, :, None, None, None]).reshape(
        (n_row,) + received.shape[1:]
    )
    returned = lax.all_to_all(spread, "row", split_axis=0, concat_axis=0, tiled=True)
    start = row_index % per_col * n_col
    owned = lax.dynamic_slice_in_dim(returned, start, n_col, 0).reshape(rows_dev, cols_dev, -1)
    col_part = owned.astype(jnp.float32)
    from_rows, grad_left = push_back(row_part, left_val, left_sig, tile_mask, left_weight, normed)
    from_cols, grad_right = push_back(
        col_part, right_val, right_sig, tile_mask, right_weight, normed
    )
    gate_back = jnp.einsum(
        "ijd,cd->ijc", gate_grad, gate_weight, preferred_element_type=jnp.float32
    )
    normed_grad = gate_back + from_rows + from_cols
    scaled = normed_grad * norm_gain
    grad_pair = (
        pair_scale
        * (
            scaled
            - jnp.mean(scaled, axis=-1, keepdims=True)
            - pair_hat * jnp.mean(scaled * pair_hat, axis=-1, keepdims=True)
        )
    ).astype(jnp.bfloat16)
    grad_norms = jnp.stack(
        [
            jnp.sum(normed_grad * pair_hat, axis=(0, 1)),
            jnp.sum(normed_grad, axis=(0, 1)),
            jnp.sum(tnorm_grad * tri_hat, axis=(0, 1)),
            jnp.sum(tnorm_grad, axis=(0, 1)),
        ]
    )
    totals = lax.psum((grad_left, grad_right, grad_gating, grad_output, grad_norms), ("row", "col"))
    inverse = 1.0 / tokens
    return (
        update,
        grad_pair,
        totals[0] * inverse,
        totals[1] * inverse,
        totals[2] * inverse,
        totals[3] * inverse,
        totals[4] * inverse,
    )


def solution(mesh):
    return jax.shard_map(
        per_device,
        mesh=mesh,
        in_specs=(
            P("row", "col", None),
            P("row", "col", None),
            P(),
            P(),
            P(),
            P(),
            P(),
            P(),
            P(),
            P(),
            P(),
        ),
        out_specs=(P("row", "col", None), P("row", "col", None), P(), P(), P(), P(), P()),
        check_vma=False,
    )
```

profile of v0, /device:TPU:0, one launch (start us, length us, event | category | flops | bytes accessed | tf_op | source)
XLA Modules:
  0.0 473.8 jit_solution(4896643660126480447)
XLA Ops:
  10.3 2.5 fusion.25
  14.4 47.0 %all-gather.2.cloned.1.call-done = bf16[32,256,128]{2,1,0:T(8,128)(2,1)} async-done(((bf16[32,64,128]{2,1,0:T(8,128)(2,1)}), bf16[32,256,128]{2,1,0:T(8,128)(2,1)}) %all-gather.2.cloned.1.call-update) | async-done | bytes 2097168 | tf_op jit(solution)/shard_map/all_gather | solution.py:75
  61.4 3.8 broadcast_select_fusion.1
  68.3 3.1 copy.54
  71.5 2.8 fusion.53
  74.4 2.7 fusion.5
  77.0 4.6 copy.52
  81.6 63.4 %all-reduce.7.cloned.1.call-done = (bf16[32,256,128]{2,1,0:T(8,128)(2,1)}, bf16[32,256,128]{2,1,0:T(8,128)(2,1)}) async-done(((bf16[32,256,128]{2,1,0:T(8,128)(2,1)}, bf16[32,256,128]{2,1,0:T(8,128)(2,1)}), (bf16[32,256,128]{2,1,0:T(8,128)(2,1)}, bf16[32,256,128]{2,1,0:T(8,128)(2,1)})) %all-reduce.7.cloned.1.call-update) | async-done | bytes 4194320 | tf_op jit(solution)/shard_map/psum | solution.py:11
  145.1 4.5 fusion.10
  149.6 4.3 fusion
  154.0 6.8 %copy.51 = bf16[64,256,128]{1,0,2:T(8,128)(2,1)} copy(bf16[64,256,128]{2,1,0:T(8,128)(2,1)} %fusion) | data formatting | bytes 8388608 | tf_op jit(solution)/shard_map/convert_element_type | solution.py:25
  160.7 4.1 bitcast_reduce_fusion
  169.9 2.2 copy.66
  173.4 4.3 fusion.75
  177.7 4.6 copy.56
  182.5 41.1 %reduce-scatter.7.cloned.1.call-done = bf16[8,32768]{1,0:T(8,128)(2,1)} async-done(((bf16[64,32768]{1,0:T(8,128)(2,1)}), bf16[8,32768]{1,0:T(8,128)(2,1)}) %reduce-scatter.7.cloned.1.call-update) | async-done | bytes 524304
  226.4 4.6 all-to-all-start
  235.7 23.9 %all-to-all-done = bf16[1,8,256,128]{3,1,0,2:T(8,128)(2,1)} async-done(((bf16[1,8,256,128]{3,1,0,2:T(8,128)(2,1)}), bf16[1,8,256,128]{3,1,0,2:T(8,128)(2,1)}, u32[]{:S(2)}, u32[]{:S(2)}) %all-to-all-start) | async-done | bytes 524320 | tf_op jit(solution)/shard_map/all_to_all | solution.py:122
  261.9 4.2 all-to-all-start.1
  269.7 11.9 %all-to-all-done.1 = bf16[8,8,64,128]{3,2,1,0:T(8,128)(2,1)} async-done(((bf16[8,8,64,128]{3,2,1,0:T(8,128)(2,1)}), bf16[8,8,64,128]{3,2,1,0:T(8,128)(2,1)}, u32[]{:S(2)}, u32[]{:S(2)}) %all-to-all-start.1) | async-done | bytes 1048608 | tf_op jit(solution)/shard_map/all_to_all | solution.py:127
  282.7 2.8 fusion.49
  289.0 2.6 fusion.30
  291.6 37.2 %psum.55 = f32[4,128]{1,0:T(4,128)S(1)} all-reduce(f32[4,128]{1,0:T(4,128)S(1)} %pad_maximum_fusion.6), channel_id=1, replica_groups=mesh['row'=8,'col'=4] {'row','col'}, use_global_device_ids=true, to_apply=%region_20.21 | all-reduce | flops 512 | bytes 4096 | tf_op jit(solution)/shard_map/psum | solution.py:156
  331.3 129.8 %all-reduce.5.cloned.1.call-done = (f32[128,256]{1,0:T(8,128)}, f32[128,256]{1,0:T(8,128)}, f32[128,128]{1,0:T(8,128)}, f32[128,128]{1,0:T(8,128)}) async-done(((f32[128,256]{1,0:T(8,128)}, f32[128,256]{1,0:T(8,128)}, f32[128,128]{1,0:T(8,128)}, f32[128,128]{1,0:T(8,128)}), (f32[128,256]{1,0:T(8,128)}, f32[128,256]{1,0:T(8,128)}, f32[128,128]{1,0:T(8,128)}, ...) | async-done | bytes 393232 | tf_op jit(solution)/shard_map/psum | solution.py:156
  (90 shorter events, 40.0 us)
Async XLA Ops:
  7.2 137.9 %copy-start = (bf16[128,256]{1,0:T(8,128)(2,1)S(1)}, bf16[128,256]{1,0:T(8,128)(2,1)}, u32[]{:S(2)}) copy-start(bf16[128,256]{1,0:T(8,128)(2,1)} %param.17) | copy-start | bytes 196612
  7.2 5.7 %copy-start.12 = (bf16[128,128]{1,0:T(8,128)(2,1)S(1)}, bf16[128,128]{1,0:T(8,128)(2,1)}, u32[]{:S(2)}) copy-start(bf16[128,128]{1,0:T(8,128)(2,1)} %param.18) | copy-start | bytes 98308
  7.2 54.2 %all-gather.2.cloned.1.call-start = ((), (), s32[]{:S(2)}) async-start(), calls=%async_computation.4 | async-start | bytes 2621440 | tf_op jit(solution)/shard_map/all_gather | solution.py:75
  12.8 132.2 %all-reduce.7.cloned.1.call-start = ((), (), s32[]{:S(2)}) async-start(), calls=%async_computation.8 | async-start | bytes 8388608 | tf_op jit(solution)/shard_map/psum | solution.py:11
  65.2 1.0 copy-start.6
  65.2 1.0 copy-start.11
  65.2 158.4 %reduce-scatter.7.cloned.1.call-start = ((), (), s32[]{:S(2)}) async-start(), calls=%async_computation.6 | async-start | bytes 4718592
  67.6 4.0 copy-start.9
  164.8 0.7 copy-start.14
  165.5 1.3 copy-start.15
  166.8 1.8 copy-start.1
  168.6 1.3 copy-start.3
  172.2 1.2 copy-start.4
  172.2 110.4 %reduce-scatter.5.cloned.1.call-start = ((), (), s32[]{:S(2)}) async-start(), calls=%async_computation.5 | async-start | bytes 2621440 | tf_op jit(solution)/shard_map/reduce_scatter | solution.py:115
  223.6 7.5 %copy-start.2 = (bf16[32,64,128]{2,1,0:T(8,128)(2,1)S(1)}, bf16[32,64,128]{2,1,0:T(8,128)(2,1)}, u32[]{:S(2)}) copy-start(bf16[32,64,128]{2,1,0:T(8,128)(2,1)} %fusion.25) | copy-start | bytes 1572868
  226.4 33.2 %all-to-all-start = ((bf16[1,8,256,128]{3,1,0,2:T(8,128)(2,1)}), bf16[1,8,256,128]{3,1,0,2:T(8,128)(2,1)}, u32[]{:S(2)}, u32[]{:S(2)}) async-start(bf16[1,8,256,128]{3,1,0,2:T(8,128)(2,1)} %copy.58), calls=%async_computation.1 | async-start | bytes 1048576 | tf_op jit(solution)/shard_map/all_to_all | solution.py:122
  231.1 3.5 copy-start.8
  260.8 5.4 %copy-start.7 = (bf16[32,64,128]{2,1,0:T(8,128)(2,1)S(1)}, bf16[32,64,128]{2,1,0:T(8,128)(2,1)}, u32[]{:S(2)}) copy-start(bf16[32,64,128]{2,1,0:T(8,128)(2,1)} %param.12) | copy-start | bytes 1572868
  261.9 19.6 %all-to-all-start.1 = ((bf16[8,8,64,128]{3,2,1,0:T(8,128)(2,1)}), bf16[8,8,64,128]{3,2,1,0:T(8,128)(2,1)}, u32[]{:S(2)}, u32[]{:S(2)}) async-start(bf16[8,8,64,128]{3,2,1,0:T(8,128)(2,1)} %bitcast_multiply_fusion), calls=%async_computation.2 | async-start | bytes 2097152 | tf_op jit(solution)/shard_map/all_to_all | solution.py:127
  266.2 195.0 %all-reduce.5.cloned.1.call-start = ((), (), s32[]{:S(2)}) async-start(), calls=%async_computation.7 | async-start | bytes 786432 | tf_op jit(solution)/shard_map/psum | solution.py:156
  285.5 2.5 copy-start.10
  286.5 2.5 copy-start.5
  286.5 2.5 copy-start.13
Sparse Core Ops, SparseCore 0:
  13.0 48.3 all-gather.1
  65.4 79.6 all-reduce.6
  172.3 51.2 reduce-scatter.6
  225.7 51.5 reduce-scatter.4
  330.9 130.2 all-reduce.4
where the time goes:
time: 475 us; the launch traced here: 474 us
  waiting for transfers between devices  317 us (67%)
  blocking collectives  37.2 us (8%)
  matrix products  32.8 us (7%)
  other arithmetic  32.6 us (7%)
  local copies, waits for them, and re-layouts  29.7 us (6%)
  between operations  14.8 us (3%)
  starting transfers between devices  9.43 us (2%)
    psum x1, waiting for transfers between devices, per_device(): lax.psum((grad_left, grad_right, grad_gating, grad_output, grad_norms), (...  130 us
    psum x1, waiting for transfers between devices, broadcast(): return lax.psum(block, axis)  63.4 us
    all_gather x1, waiting for transfers between devices, per_device(): row_panel = lax.all_gather(normed, 'col', axis=1, tiled=True)  47 us
    unnamed x6, waiting for transfers between devices  41.2 us
    psum x1, blocking collectives, per_device(): lax.psum((grad_left, grad_right, grad_gating, grad_output, grad_norms), (...  37.2 us
    all_to_all x1, waiting for transfers between devices, per_device(): lax.all_to_all(slab, 'col', split_axis=2, concat_axis=0, tiled=True)  23.9 us
    all_to_all x1, waiting for transfers between devices, per_device(): lax.all_to_all(spread, 'row', split_axis=0, concat_axis=0, tiled=True)  11.9 us
    convert_element_type x2, local copies, waits for them, and re-layouts, gating(): (pad_mask * sigmoid_val * values).astype(jnp.bfloat16)  11.4 us
  transfers between devices with their start and end apart: 7, of which 6 were waited for; matrix products, arithmetic and copies ran while one was open for 8% of the time, Pallas kernels for 0%

commit v1 on v0

--- a/solution.py
+++ b/solution.py
@@ -6,9 +6,15 @@
 EPS = 1e-05
 
 
+def summed_here(array, name):
+    parts = lax.all_gather(array, name, axis=0, tiled=False)
+    result = parts.sum(axis=0)
+    return result
+
+
 def broadcast(block, axis, holder):
     block = jnp.where(lax.axis_index(axis) == holder, block, jnp.zeros_like(block))
-    return lax.psum(block, axis)
+    return summed_here(block, axis)
 
 
 def normalize(values):

time: 475 us -> 586 us (1.23)
  waiting for transfers between devices: 317 us -> 407 us
  other arithmetic: 32.6 us -> 53.6 us
    all_gather x0 -> x2, waiting for transfers between devices: none -> 152 us  [summed_here(): parts = lax.all_gather(array, name, axis=0, tiled=False)]
    psum x1 -> x0, waiting for transfers between devices: 63.4 us -> none  [broadcast(): return lax.psum(block, axis)]
    reduce_sum x0 -> x2, other arithmetic: none -> 21.1 us  [summed_here(): result = parts.sum(axis=0)]
    unnamed x6 -> x7, waiting for transfers between devices: 41.2 us -> 41.8 us
  transfers between devices with their start and end apart: 7 -> 8, of which waited for: 6 -> 7; matrix products, arithmetic and copies ran while one was open for 8% -> 9% of each run, Pallas kernels for 0% -> 0%
where the time goes in v1:
time: 586 us; the launch traced here: 584 us
  waiting for transfers between devices  407 us (69%)
  other arithmetic  53.6 us (9%)
  blocking collectives  37.2 us (6%)
  matrix products  33.2 us (6%)
  local copies, waits for them, and re-layouts  29.2 us (5%)
  between operations  15.1 us (3%)
  starting transfers between devices  9.09 us (2%)
    all_gather x2, waiting for transfers between devices, summed_here(): parts = lax.all_gather(array, name, axis=0, tiled=False)  152 us
    psum x1, waiting for transfers between devices, per_device(): lax.psum((grad_left, grad_right, grad_gating, grad_output, grad_norms), (...  130 us
    all_gather x1, waiting for transfers between devices, per_device(): row_panel = lax.all_gather(normed, 'col', axis=1, tiled=True)  48.5 us
    unnamed x7, waiting for transfers between devices  41.8 us
    psum x1, blocking collectives, per_device(): lax.psum((grad_left, grad_right, grad_gating, grad_output, grad_norms), (...  37.2 us
    all_to_all x1, waiting for transfers between devices, per_device(): lax.all_to_all(slab, 'col', split_axis=2, concat_axis=0, tiled=True)  23.8 us
    reduce_sum x2, other arithmetic, summed_here(): result = parts.sum(axis=0)  21.1 us
  transfers between devices with their start and end apart: 8, of which 7 were waited for; matrix products, arithmetic and copies ran while one was open for 9% of the time, Pallas kernels for 0%

profile of v1, /device:TPU:0, one launch (start us, length us, event | category | flops | bytes accessed | tf_op | source)
XLA Modules:
  0.0 584.5 jit_solution(9061082145251062868)
XLA Ops:
  12.9 48.5 %all-gather.6.cloned.1.call-done = bf16[32,256,128]{2,1,0:T(8,128)(2,1)} async-done(((bf16[32,64,128]{2,1,0:T(8,128)(2,1)}), bf16[32,256,128]{2,1,0:T(8,128)(2,1)}) %all-gather.6.cloned.1.call-update) | async-done | bytes 2097168 | tf_op jit(solution)/shard_map/all_gather | solution.py:81
  61.4 3.9 broadcast_select_fusion.1
  69.1 3.1 copy.54
  72.4 3.1 fusion.53
  75.5 2.9 fusion.5
  78.4 4.6 copy.52
  83.0 71.0 %all-gather.8.cloned.1.call-done = bf16[256,256,128]{2,1,0:T(8,128)(2,1)} async-done(((bf16[32,256,128]{2,1,0:T(8,128)(2,1)}), bf16[256,256,128]{2,1,0:T(8,128)(2,1)}) %all-gather.8.cloned.1.call-update) | async-done | bytes 16777232 | tf_op jit(solution)/shard_map/all_gather | solution.py:10
  154.0 10.6 %reduce_sum.134 = bf16[32,256,128]{2,1,0:T(8,128)(2,1)} reduce(bf16[8,32,256,128]{3,2,1,0:T(8,128)(2,1)} %bitcast.113, bf16[]{:T(256)} %constant.61.clone.1), dimensions={0}, to_apply=%region_2.3 | reduce | flops 7340032 | bytes 18874370 | tf_op jit(solution)/shard_map/reduce_sum | solution.py:11
  164.6 81.1 %all-gather.10.cloned.1.call-done = bf16[256,256,128]{2,1,0:T(8,128)(2,1)} async-done(((bf16[32,256,128]{2,1,0:T(8,128)(2,1)}), bf16[256,256,128]{2,1,0:T(8,128)(2,1)}) %all-gather.10.cloned.1.call-update) | async-done | bytes 16777232 | tf_op jit(solution)/shard_map/all_gather | solution.py:10
  245.7 10.5 %reduce_sum.135 = bf16[32,256,128]{2,1,0:T(8,128)(2,1)} reduce(bf16[8,32,256,128]{3,2,1,0:T(8,128)(2,1)} %bitcast.114, bf16[]{:T(256)} %constant.61.clone.1), dimensions={0}, to_apply=%region_3.4 | reduce | flops 7340032 | bytes 18874370 | tf_op jit(solution)/shard_map/reduce_sum | solution.py:11
  256.2 4.5 fusion.10
  260.7 4.3 fusion
  265.1 6.8 %copy.51 = bf16[64,256,128]{1,0,2:T(8,128)(2,1)} copy(bf16[64,256,128]{2,1,0:T(8,128)(2,1)} %fusion) | data formatting | bytes 8388608 | tf_op jit(solution)/shard_map/convert_element_type | solution.py:31
  271.9 4.1 bitcast_reduce_fusion
  284.5 4.3 fusion.75
  288.8 4.6 copy.56
  293.6 41.1 %reduce-scatter.7.cloned.1.call-done = bf16[8,32768]{1,0:T(8,128)(2,1)} async-done(((bf16[64,32768]{1,0:T(8,128)(2,1)}), bf16[8,32768]{1,0:T(8,128)(2,1)}) %reduce-scatter.7.cloned.1.call-update) | async-done | bytes 524304
  337.4 4.6 all-to-all-start
  346.7 23.8 %all-to-all-done = bf16[1,8,256,128]{3,1,0,2:T(8,128)(2,1)S(1)} async-done(((bf16[1,8,256,128]{3,1,0,2:T(8,128)(2,1)}), bf16[1,8,256,128]{3,1,0,2:T(8,128)(2,1)S(1)}, u32[]{:S(2)}, u32[]{:S(2)}) %all-to-all-start) | async-done | bytes 524320 | tf_op jit(solution)/shard_map/all_to_all | solution.py:128
  371.9 4.2 all-to-all-start.1
  380.6 10.9 %all-to-all-done.1 = bf16[8,8,64,128]{3,2,1,0:T(8,128)(2,1)} async-done(((bf16[8,8,64,128]{3,2,1,0:T(8,128)(2,1)}), bf16[8,8,64,128]{3,2,1,0:T(8,128)(2,1)}, u32[]{:S(2)}, u32[]{:S(2)}) %all-to-all-start.1) | async-done | bytes 1048608 | tf_op jit(solution)/shard_map/all_to_all | solution.py:133
  399.1 2.7 fusion.30
  401.9 37.2 %psum.39 = f32[4,128]{1,0:T(4,128)S(1)} all-reduce(f32[4,128]{1,0:T(4,128)S(1)} %pad_maximum_fusion.6), channel_id=1, replica_groups=mesh['row'=8,'col'=4] {'row','col'}, use_global_device_ids=true, to_apply=%region_20.21 | all-reduce | flops 512 | bytes 4096 | tf_op jit(solution)/shard_map/psum | solution.py:162
  441.6 129.9 %all-reduce.3.cloned.1.call-done = (f32[128,256]{1,0:T(8,128)}, f32[128,256]{1,0:T(8,128)}, f32[128,128]{1,0:T(8,128)}, f32[128,128]{1,0:T(8,128)}) async-done(((f32[128,256]{1,0:T(8,128)}, f32[128,256]{1,0:T(8,128)}, f32[128,128]{1,0:T(8,128)}, f32[128,128]{1,0:T(8,128)}), (f32[128,256]{1,0:T(8,128)}, f32[128,256]{1,0:T(8,128)}, f32[128,128]{1,0:T(8,128)}, ...) | async-done | bytes 393232 | tf_op jit(solution)/shard_map/psum | solution.py:162
  (103 shorter events, 47.1 us)
Async XLA Ops:
  7.2 249.0 %copy-start = (bf16[128,256]{1,0:T(8,128)(2,1)S(1)}, bf16[128,256]{1,0:T(8,128)(2,1)}, u32[]{:S(2)}) copy-start(bf16[128,256]{1,0:T(8,128)(2,1)} %param.17) | copy-start | bytes 196612
  7.2 54.2 %all-gather.6.cloned.1.call-start = ((), (), s32[]{:S(2)}) async-start(), calls=%async_computation.4 | async-start | bytes 2621440 | tf_op jit(solution)/shard_map/all_gather | solution.py:81
  12.8 141.2 %all-gather.8.cloned.1.call-start = ((), (), s32[]{:S(2)}) async-start(), calls=%async_computation.6 | async-start | bytes 18874368 | tf_op jit(solution)/shard_map/all_gather | solution.py:10
  65.2 1.5 copy-start.2
  65.2 1.5 copy-start.16
  65.2 180.4 %all-gather.10.cloned.1.call-start = ((), (), s32[]{:S(2)}) async-start(), calls=%async_computation.7 | async-start | bytes 18874368 | tf_op jit(solution)/shard_map/all_gather | solution.py:10
  66.0 268.7 %reduce-scatter.7.cloned.1.call-start = ((), (), s32[]{:S(2)}) async-start(), calls=%async_computation.8 | async-start | bytes 4718592
  67.7 1.3 copy-start.3
  69.1 3.3 copy-start.12
  276.6 1.3 copy-start.19
  277.9 1.8 copy-start.1
  279.7 1.3 copy-start.5
  283.3 109.3 %reduce-scatter.5.cloned.1.call-start = ((), (), s32[]{:S(2)}) async-start(), calls=%async_computation.5 | async-start | bytes 2621440 | tf_op jit(solution)/shard_map/reduce_scatter | solution.py:121
  337.4 33.1 %all-to-all-start = ((bf16[1,8,256,128]{3,1,0,2:T(8,128)(2,1)}), bf16[1,8,256,128]{3,1,0,2:T(8,128)(2,1)S(1)}, u32[]{:S(2)}, u32[]{:S(2)}) async-start(bf16[1,8,256,128]{3,1,0,2:T(8,128)(2,1)} %copy.58), calls=%async_computation.1 | async-start | bytes 1048576 | tf_op jit(solution)/shard_map/all_to_all | solution.py:128
  342.1 3.5 copy-start.11
  370.6 5.5 copy-start.4
  371.9 19.6 %all-to-all-start.1 = ((bf16[8,8,64,128]{3,2,1,0:T(8,128)(2,1)}), bf16[8,8,64,128]{3,2,1,0:T(8,128)(2,1)}, u32[]{:S(2)}, u32[]{:S(2)}) async-start(bf16[8,8,64,128]{3,2,1,0:T(8,128)(2,1)} %bitcast_multiply_fusion), calls=%async_computation.2 | async-start | bytes 2097152 | tf_op jit(solution)/shard_map/all_to_all | solution.py:133
  376.1 195.4 %all-reduce.3.cloned.1.call-start = ((), (), s32[]{:S(2)}) async-start(), calls=%async_computation.9 | async-start | bytes 786432 | tf_op jit(solution)/shard_map/psum | solution.py:162
  379.3 13.3 %copy-start.7 = (f32[32,64,256]{2,1,0:T(8,128)S(1)}, f32[32,64,256]{2,1,0:T(8,128)}, u32[]{:S(2)}) copy-start(f32[32,64,256]{2,1,0:T(8,128)} %fusion.51) | copy-start | bytes 6291460
  395.0 3.1 copy-start.13
  395.0 3.1 copy-start.14
  395.0 1.6 copy-start.10
  396.7 2.5 copy-start.8
  396.7 2.5 copy-start.17
  (4 other events, 4.0 us)
Sparse Core Ops, SparseCore 0:
  12.9 48.3 all-gather.5
  65.4 88.5 all-gather.7
  155.9 89.7 all-gather.9
  283.5 51.1 reduce-scatter.6
  336.8 51.5 reduce-scatter.4
  441.2 130.3 all-reduce.2
